TPU v7x, 32 devices: a whole 2x2x4 slice. The times are simulated.
32 devices in a mesh: section: 8 (over y, x, core), tensor: 4 (over z).
Axes of the slice: x: 2, y: 2, z: 4, core: 2. Of those that a mesh axis runs over, the one named last changes fastest.
Arguments:
- frozen: bfloat16 [8, 14336, 2048], P('section', 'tensor'), may hold values from -1 to 1, as said below
- adapter_a: bfloat16 [8, 8, 14336], P('section', None, 'tensor'), may hold values from -0.119628906 to 0.119628906
- adapter_b: bfloat16 [8, 16, 2048], P('section'), may hold values from -0.22460938 to 0.22460938
- magnitude: float32 [8, 2048], P('section'), may hold values from 0.5 to 2
- hidden_fwd: bfloat16 [8, 128, 14336], P('section', None, 'tensor'), may hold values from -6 to 6
- carried: bfloat16 [8, 256, 2048], P('section', 'tensor'), may hold values from -6 to 6
- embedded: bfloat16 [256, 4096], P('tensor'), may hold values from -6 to 6
- hidden_bwd: bfloat16 [8, 128, 14336], P('section', None, 'tensor'), may hold values from -6 to 6
- returned: bfloat16 [8, 256, 2048], P('section', 'tensor'), may hold values from -1.5 to 1.5
- head_grad: bfloat16 [256, 4096], P('tensor'), may hold values from -1.5 to 1.5
Outputs:
- section_out: bfloat16 [8, 256, 2048], P('section', 'tensor')
- grad_magnitude: float32 [8, 2048], P('section')
- grad_a: float32 [8, 8, 14336], P('section', None, 'tensor')
- grad_b: float32 [8, 16, 2048], P('section')
- hidden_grad: bfloat16 [8, 128, 14336], P('section', None, 'tensor')
Inputs may be any that keep to these rules, and one draw needn't show every extreme that they name: frozen projection weights.
All inputs are finite; a program needn't handle non-finite values.
Results may differ from a plain program's by a relative error of at most 0.0057.
Values may be sent and summed in bfloat16 or wider, within the bound.
No kernel may reach another device: no remote copies, remote signals or barrier semaphores. Data moves between devices by JAX's collectives and lax.ppermute only.
A program may use at most 128 MiB of HBM per device.

v0:
```python
import jax
import jax.numpy as jnp
from jax import lax
from jax.sharding import PartitionSpec as P

epsilon = 1e-06


def swapped(array, axis, apart):
    return lax.ppermute(array, axis, [(i, i ^ 1 << apart) for i in range(lax.axis_size(axis))])


def from_behind(array, axis, by):
    count = lax.axis_size(axis)
    pairs = [(i, i + by) for i in range(count) if 0 <= i + by < count]
    return lax.ppermute(array, axis, pairs)


def column_norms(squares):
    return jnp.sqrt(lax.psum(squares, "tensor") + epsilon)


def forward_rows(term_fn, own_rows):
    return lax.psum_scatter(
        term_fn(jnp.int32(0), own_rows * lax.axis_size("tensor")),
        "tensor",
        scatter_dimension=0,
        tiled=True,
    )


def local(
    frozen,
    adapter_a,
    adapter_b,
    magnitude,
    hidden_fwd,
    carried,
    embedded,
    hidden_bwd,
    returned,
    head_grad,
):
    base_w = frozen[0]
    fac_half = adapter_a[0]
    fac_b = adapter_b[0]
    mag = magnitude[0]
    own_rows = carried.shape[1]
    slot_id = lax.axis_index("section")
    slot_count = lax.axis_size("section")
    half = slot_id % 2
    first_half = half == 0
    fwd_other, bwd_other, fac_other = swapped(
        (hidden_fwd[0], hidden_bwd[0], fac_half), "section", 0
    )

    def in_order(own, other):
        return jnp.concatenate(
            [jnp.where(first_half, own, other), jnp.where(first_half, other, own)], axis=0
        )

    hid_fwd = in_order(hidden_fwd[0], fwd_other)
    hid_bwd = in_order(hidden_bwd[0], bwd_other)
    fac_a = in_order(fac_half, fac_other)
    width = base_w.shape[1]
    arriving = from_behind(carried[0], "section", 2)
    embed_cols = lax.dynamic_slice_in_dim(embedded, half * width, width, 1)
    inflow = jnp.where(slot_id < 2, embed_cols, arriving)
    coming = from_behind(returned[0], "section", -2)
    head_cols = lax.dynamic_slice_in_dim(head_grad, half * width, width, 1)
    cotangent = jnp.where(slot_id >= slot_count - 2, head_cols, coming)
    merged = (
        base_w.astype(jnp.float32)
        + jnp.einsum("rf,rd->fd", fac_a, fac_b, preferred_element_type=jnp.float32)
    ).astype(jnp.bfloat16)
    merged_f = merged.astype(jnp.float32)
    squares = jnp.sum(merged_f * merged_f, axis=0)
    low_part = jnp.einsum("tf,rf->tr", hid_bwd, fac_a, preferred_element_type=jnp.float32)
    low = lax.psum(low_part, "tensor").astype(jnp.bfloat16)
    col_norms = column_norms(squares)
    col_scale = mag / col_norms

    def scaled_term(offset, amount):
        return jnp.dot(hid_fwd, merged, preferred_element_type=jnp.float32) * col_scale

    projected = forward_rows(scaled_term, own_rows)
    section_out = (inflow.astype(jnp.float32) + projected).astype(jnp.bfloat16)
    all_rows = hid_bwd.shape[0]
    cot_block = lax.all_gather(cotangent, "tensor", axis=0, tiled=True)
    scaled_cot = (cot_block.astype(jnp.float32) * col_scale).astype(jnp.bfloat16)
    hid_part = jnp.einsum("td,fd->tf", scaled_cot, merged, preferred_element_type=jnp.float32)
    hid_acc = hid_part
    adapt_part = jnp.einsum("td,rd->tr", scaled_cot, fac_b, preferred_element_type=jnp.float32)
    adapt_acc = adapt_part
    grad_b_acc = jnp.einsum("tr,td->rd", low, scaled_cot, preferred_element_type=jnp.float32)
    recomputed = jnp.dot(hid_bwd, merged, preferred_element_type=jnp.float32)
    mag_acc = jnp.sum(cot_block.astype(jnp.float32) * recomputed, axis=0)
    hid_acc, adapt_acc, grad_b_acc, mag_acc = (hid_acc, adapt_acc, grad_b_acc, mag_acc)
    half_rows = all_rows // 2
    send_hid = lax.dynamic_slice_in_dim(hid_acc, (1 - half) * half_rows, half_rows, 0)
    got_hid, got_adapt = swapped((send_hid, adapt_acc), "section", 0)
    own_hid = lax.dynamic_slice_in_dim(hid_acc, half * half_rows, half_rows, 0)
    hidden_grad = (own_hid + got_hid).astype(jnp.bfloat16)
    adapter_cot = (adapt_acc + got_adapt).astype(jnp.bfloat16)
    rank_half = fac_half.shape[0]
    own_cot = lax.dynamic_slice_in_dim(adapter_cot, half * rank_half, rank_half, 1)
    grad_a = jnp.einsum("tr,tf->rf", own_cot, hid_bwd, preferred_element_type=jnp.float32)
    grad_mag = lax.psum(mag_acc, "tensor") / col_norms
    return (section_out[None], grad_mag[None], grad_a[None], grad_b_acc[None], hidden_grad[None])


def solution(mesh):
    placed = (
        P("section", "tensor", None),
        P("section", None, "tensor"),
        P("section", None, None),
        P("section", None),
        P("section", None, "tensor"),
        P("section", "tensor", None),
        P("tensor", None),
        P("section", None, "tensor"),
        P("section", "tensor", None),
        P("tensor", None),
    )
    return jax.shard_map(
        local,
        mesh=mesh,
        in_specs=placed,
        out_specs=(
            P("section", "tensor", None),
            P("section", None),
            P("section", None, "tensor"),
            P("section", None, None),
            P("section", None, "tensor"),
        ),
        check_vma=False,
    )
```

profile of v0, /device:TPU:0, one launch (start us, length us, event | category | flops | bytes accessed | tf_op | source)
XLA Modules:
  0.0 143.7 jit_solution(12849420476507222453)
XLA Ops:
  7.9 1.3 collective-permute-start.3
  9.7 0.8 broadcast_select_fusion.5
  10.5 11.0 %multiply_reduce_fusion = (f32[2048]{0:T(1024)S(1)}, bf16[3584,2048]{1,0:T(8,128)(2,1)}) fusion(bf16[1,16,2048]{2,1,0:T(8,128)(2,1)S(1)} %copy-done, bf16[8,3584]{1,0:T(8,128)(2,1)S(1)} %get-tuple-element.13, bf16[8,3584]{1,0:T(8,128)(2,1)S(1)} %get-tuple-element.12, bf16[1,3584,2048]{2,1,0:T(8,128)(2,1)} %param.10), kind=kOutput, calls=%fused_computation.2 | convolution fusion | flops 279148544 | bytes 29548544 | tf_op jit(solution)/shard_map/rf,rd->fd/dot_general | solution.py:74
  21.5 0.8 dynamic-slice_select_fusion
  22.4 1.3 broadcast_select_fusion.1
  23.7 0.6 fusion.12
  24.6 0.9 copy-done.5
  25.5 1.0 broadcast_select_fusion.3
  26.6 27.4 %all-gather.2.cloned.1.call-done = bf16[256,2048]{1,0:T(8,128)(2,1)} async-done(((bf16[64,2048]{1,0:T(8,128)(2,1)}), bf16[256,2048]{1,0:T(8,128)(2,1)}) %all-gather.2.cloned.1.call-update) | async-done | bytes 1048592 | tf_op jit(solution)/shard_map/all_gather | solution.py:89
  54.0 9.7 %fusion.5 = f32[2048]{0:T(1024)S(1)} fusion(bf16[3584,2048]{1,0:T(8,128)(2,1)} %get-tuple-element.17, bf16[256,2048]{1,0:T(8,128)(2,1)} %all-gather.2.cloned.1.call-done, bf16[128,3584]{1,0:T(8,128)(2,1)} %copy-done.8, bf16[128,3584]{1,0:T(8,128)(2,1)S(1)} %get-tuple-element.8), kind=kOutput, calls=%fused_computation.14 | convolution fusion | flops 3763337216 | bytes 17571840 | tf_op jit(solution)/shard_map/dot_general | solution.py:96
  63.7 19.6 %all-reduce = (f32[2048]{0:T(1024)S(1)}, f32[2048]{0:T(1024)S(1)}, bf16[256,16]{1,0:T(8,128)(2,1)S(1)}) all-reduce(f32[2048]{0:T(1024)S(1)} %get-tuple-element.16, f32[2048]{0:T(1024)S(1)} %fusion.5, f32[256,16]{1,0:T(8,128)S(1)} %fusion.12), channel_id=1, replica_groups=mesh['section'=8,'tensor'=4] {'tensor'}, use_global_device_ids=true, to_apply=%region_1.2 | all-reduce | flops 8192 | bytes 57344 | tf_op jit(solution)/shard_map/psum | solution.py:20
  83.3 0.6 fusion.18
  83.9 8.9 %convolution_multiply_fusion.1 = f32[256,2048]{1,0:T(8,128)} fusion(bf16[3584,2048]{1,0:T(8,128)(2,1)} %get-tuple-element.17, bf16[128,3584]{1,0:T(8,128)(2,1)S(1)} %copy-done.9, bf16[128,3584]{1,0:T(8,128)(2,1)S(1)} %get-tuple-element.10, f32[2048]{0:T(1024)S(1)} %get-tuple-element.15), kind=kOutput, calls=%fused_computation.5 | convolution fusion | flops 3762290688 | bytes 18620416 | tf_op jit(solution)/shard_map/dot_general | solution.py:84
  92.9 1.2 copy-done.3
  94.1 7.7 %fusion.7 = f32[256,3584]{1,0:T(8,128)S(1)} fusion(bf16[3584,2048]{1,0:T(8,128)(2,1)} %get-tuple-element.17, bf16[256,2048]{1,0:T(8,128)(2,1)S(1)} %copy-done.3, f32[2048]{0:T(1024)S(1)} %get-tuple-element.15), kind=kOutput, calls=%fused_computation.20 | convolution fusion | flops 3759669248 | bytes 19406848 | tf_op jit(solution)/shard_map/td,fd->tf/dot_general | solution.py:91
  101.8 1.8 %copy-done.1 = f32[256,3584]{1,0:T(8,128)} copy-done((f32[256,3584]{1,0:T(8,128)}, f32[256,3584]{1,0:T(8,128)S(1)}, u32[]{:S(2)}) %copy-start.1) | copy-done | bytes 3670040
  103.6 1.4 constant_dynamic-slice_fusion
  105.0 3.4 %collective-permute-start = (bf16[64,2048]{1,0:T(8,128)(2,1)S(1)}, bf16[64,2048]{1,0:T(8,128)(2,1)S(1)}, u32[]{:S(2)}, u32[]{:S(2)}) collective-permute-start(bf16[64,2048]{1,0:T(8,128)(2,1)S(1)} %bitcast.41), channel_id=1, source_target_pairs={{0,8},{4,12},{8,16},{12,20},{16,24},{20,28},{1,9},{5,13},{9,17},{1... | collective-permute-start | bytes 786440 | tf_op jit(solution)/shard_map/ppermute | solution.py:16
  109.0 0.9 convolution_bitcast_fusion.1
  109.9 2.2 %convolution_bitcast_fusion = f32[1,8,3584]{2,1,0:T(8,128)} fusion(bf16[128,3584]{1,0:T(8,128)(2,1)} %copy-done.8, bf16[128,3584]{1,0:T(8,128)(2,1)S(1)} %copy-done.7, f32[256,16]{0,1:T(8,128)S(1)} %collective-permute-done.5, s32[]{:T(128)S(6)} %select_n.80, f32[256,16]{0,1:T(8,128)S(1)} %fusion.10), kind=kOutput, calls=%fused_computation.3 | convolution fusion | flops 18354176 | bytes 1966084 | tf_op jit(solution)/shard_map/tr,tf->rf/dot_general | solution.py:107
  112.2 1.2 fusion.6
  113.3 1.2 collective-permute-done
  114.5 20.4 %reduce-scatter.2.cloned.1.call-done = f32[64,2048]{1,0:T(8,128)} async-done(((f32[256,2048]{1,0:T(8,128)}), f32[64,2048]{1,0:T(8,128)}) %reduce-scatter.2.cloned.1.call-update) | async-done | bytes 524304 | tf_op jit(solution)/shard_map/reduce_scatter | solution.py:24
  135.0 1.8 %fusion.13 = bf16[1,64,2048]{2,1,0:T(8,128)(2,1)} fusion(f32[64,2048]{1,0:T(8,128)} %reduce-scatter.2.cloned.1.call-done, bf16[64,2048]{1,0:T(8,128)(2,1)S(1)} %collective-permute-done, bf16[64,4096]{1,0:T(8,128)(2,1)S(1)} %copy-done.11, s32[]{:T(128)S(6)} %select_n.68, pred[]{:T(512)S(6)} %lt.22), kind=kLoop, calls=%fused_computation.24 | loop fusion | flops 524288 | bytes 1310725 | tf_op jit(solution)/shard_map/broadcast_in_dim | solution.py:109
  (41 shorter events, 2.2 us)
Async XLA Ops:
  7.2 3.3 %copy-start = (bf16[1,16,2048]{2,1,0:T(8,128)(2,1)S(1)}, bf16[1,16,2048]{2,1,0:T(8,128)(2,1)}, u32[]{:S(2)}) copy-start(bf16[1,16,2048]{2,1,0:T(8,128)(2,1)} %param.12) | copy-start | bytes 196612
  7.2 46.8 %all-gather.2.cloned.1.call-start = ((), (), s32[]{:S(2)}) async-start(), calls=%async_computation.2 | async-start | bytes 1310720 | tf_op jit(solution)/shard_map/all_gather | solution.py:89
  7.2 2.4 %collective-permute-start.2 = (bf16[8,3584]{1,0:T(8,128)(2,1)}, bf16[8,3584]{1,0:T(8,128)(2,1)S(1)}, u32[]{:S(2)}, u32[]{:S(2)}) collective-permute-start(bf16[8,3584]{1,0:T(8,128)(2,1)} %bitcast.37), channel_id=1, source_target_pairs={{0,4},{4,0},{8,12},{12,8},{16,20},{20,16},{24,28},{28,24},{1,5},{5... | collective-permute-start | bytes 172040 | tf_op jit(solution)/shard_map/ppermute | solution.py:10
  7.8 16.5 %collective-permute-start.1 = (bf16[128,3584]{1,0:T(8,128)(2,1)}, bf16[128,3584]{1,0:T(8,128)(2,1)S(1)}, u32[]{:S(2)}, u32[]{:S(2)}) collective-permute-start(bf16[128,3584]{1,0:T(8,128)(2,1)} %bitcast.36), channel_id=1, source_target_pairs={{0,4},{4,0},{8,12},{12,8},{16,20},{20,16},{24,28},{28,24},{1,5},{5... | collective-permute-start | bytes 2752520 | tf_op jit(solution)/shard_map/ppermute | solution.py:10
  7.9 13.6 %collective-permute-start.3 = (bf16[64,2048]{1,0:T(8,128)(2,1)}, bf16[64,2048]{1,0:T(8,128)(2,1)S(1)}, u32[]{:S(2)}, u32[]{:S(2)}) collective-permute-start(bf16[64,2048]{1,0:T(8,128)(2,1)} %bitcast.40), channel_id=1, source_target_pairs={{8,0},{12,4},{16,8},{20,12},{24,16},{28,20},{9,1},{13,5},{17,9},{2... | collective-permute-start | bytes 786440 | tf_op jit(solution)/shard_map/ppermute | solution.py:16
  9.2 13.2 %collective-permute-start.4 = (bf16[128,3584]{1,0:T(8,128)(2,1)}, bf16[128,3584]{1,0:T(8,128)(2,1)}, u32[]{:S(2)}, u32[]{:S(2)}) collective-permute-start(bf16[128,3584]{1,0:T(8,128)(2,1)} %bitcast.35), channel_id=1, source_target_pairs={{0,4},{4,0},{8,12},{12,8},{16,20},{20,16},{24,28},{28,24},{1,5},{5... | collective-permute-start | bytes 2752520 | tf_op jit(solution)/shard_map/ppermute | solution.py:10
  10.5 11.0 %copy-start.10 = (bf16[64,4096]{1,0:T(8,128)(2,1)S(1)}, bf16[64,4096]{1,0:T(8,128)(2,1)}, u32[]{:S(2)}) copy-start(bf16[64,4096]{1,0:T(8,128)(2,1)} %param.19) | copy-start | bytes 1572868
  10.5 11.8 %copy-start.4 = (bf16[1,128,3584]{2,1,0:T(8,128)(2,1)S(1)}, bf16[1,128,3584]{2,1,0:T(8,128)(2,1)}, u32[]{:S(2)}) copy-start(bf16[1,128,3584]{2,1,0:T(8,128)(2,1)} %param.17) | copy-start | bytes 2752516
  22.3 112.7 %reduce-scatter.2.cloned.1.call-start = ((), (), s32[]{:S(2)}) async-start(), calls=%async_computation.1 | async-start | bytes 2621440 | tf_op jit(solution)/shard_map/reduce_scatter | solution.py:24
  23.7 0.9 copy-start.8
  23.7 30.3 %copy-start.6 = (bf16[128,3584]{1,0:T(8,128)(2,1)}, bf16[128,3584]{1,0:T(8,128)(2,1)S(1)}, u32[]{:S(2)}) copy-start(bf16[128,3584]{1,0:T(8,128)(2,1)S(1)} %get-tuple-element.8) | copy-start | bytes 2752516
  23.7 1.8 %copy-start.5 = (bf16[1,128,3584]{2,1,0:T(8,128)(2,1)S(1)}, bf16[1,128,3584]{2,1,0:T(8,128)(2,1)}, u32[]{:S(2)}) copy-start(bf16[1,128,3584]{2,1,0:T(8,128)(2,1)} %param.14) | copy-start | bytes 2752516
  54.0 29.3 %copy-start.12 = (f32[1,2048]{1,0:T(1,128)S(1)}, f32[1,2048]{1,0:T(1,128)}, u32[]{:S(2)}) copy-start(f32[1,2048]{1,0:T(1,128)} %param.13) | copy-start | bytes 24580
  54.0 30.0 %copy-start.9 = (bf16[128,3584]{1,0:T(8,128)(2,1)S(1)}, bf16[128,3584]{1,0:T(8,128)(2,1)}, u32[]{:S(2)}) copy-start(bf16[128,3584]{1,0:T(8,128)(2,1)} %get-tuple-element.11) | copy-start | bytes 2752516
  92.9 1.2 copy-start.3
  101.8 1.8 %copy-start.1 = (f32[256,3584]{1,0:T(8,128)}, f32[256,3584]{1,0:T(8,128)S(1)}, u32[]{:S(2)}) copy-start(f32[256,3584]{1,0:T(8,128)S(1)} %fusion.7) | copy-start | bytes 11010052
  103.6 1.4 copy-start.13
  104.9 7.2 %collective-permute-start.6 = (f32[128,3584]{1,0:T(8,128)}, f32[128,3584]{1,0:T(8,128)S(1)}, u32[]{:S(2)}, u32[]{:S(2)}) collective-permute-start(f32[128,3584]{1,0:T(8,128)} %constant_dynamic-slice_fusion), channel_id=1, source_target_pairs={{0,4},{4,0},{8,12},{12,8},{16,20},{20,16},{24,28},{28,24},{1,5},{5... | collective-permute-start | bytes 5505032 | tf_op jit(solution)/shard_map/ppermute | solution.py:10
  105.0 9.6 %collective-permute-start = (bf16[64,2048]{1,0:T(8,128)(2,1)S(1)}, bf16[64,2048]{1,0:T(8,128)(2,1)S(1)}, u32[]{:S(2)}, u32[]{:S(2)}) collective-permute-start(bf16[64,2048]{1,0:T(8,128)(2,1)S(1)} %bitcast.41), channel_id=1, source_target_pairs={{0,8},{4,12},{8,16},{12,20},{16,24},{20,28},{1,9},{5,13},{9,17},{1... | collective-permute-start | bytes 786440 | tf_op jit(solution)/shard_map/ppermute | solution.py:16
  108.4 1.6 %copy-start.7 = (bf16[128,3584]{1,0:T(8,128)(2,1)S(1)}, bf16[128,3584]{1,0:T(8,128)(2,1)}, u32[]{:S(2)}) copy-start(bf16[128,3584]{1,0:T(8,128)(2,1)} %copy-done.6) | copy-start | bytes 2752516
  108.7 3.4 %copy-start.2 = (f32[256,3584]{1,0:T(8,128)S(1)}, f32[256,3584]{1,0:T(8,128)}, u32[]{:S(2)}) copy-start(f32[256,3584]{1,0:T(8,128)} %copy-done.1) | copy-start | bytes 11010052
  108.7 1.2 collective-permute-start.5
  112.1 22.8 %copy-start.11 = (bf16[64,4096]{1,0:T(8,128)(2,1)S(1)}, bf16[64,4096]{1,0:T(8,128)(2,1)}, u32[]{:S(2)}) copy-start(bf16[64,4096]{1,0:T(8,128)(2,1)} %param.16) | copy-start | bytes 1572868
Sparse Core Ops, SparseCore 0:
  22.4 31.5 all-gather.1
  93.0 41.9 reduce-scatter.1
where the time goes:
time: 144 us
  waiting for transfers between devices  49.1 us (34%)
  matrix products  41.4 us (29%)
  blocking collectives  19.6 us (14%)
  between operations  14.2 us (10%)
  other arithmetic  7.57 us (5%)
  starting transfers between devices  6.09 us (4%)
  local copies, waits for them, and re-layouts  5.62 us (4%)
    all_gather x1, waiting for transfers between devices, local(): cot_block = lax.all_gather(cotangent, 'tensor', axis=0, tiled=True)  27.4 us
    reduce_scatter x1, waiting for transfers between devices, forward_rows(): lax.psum_scatter(term_fn(jnp.int32(0), own_rows * lax.axis_size('tensor')...  20.4 us
    psum x1, blocking collectives, column_norms(): return jnp.sqrt(lax.psum(squares, 'tensor') + epsilon)  19.6 us
    dot_general x1, matrix products, local(): jnp.einsum('rf,rd->fd', fac_a, fac_b, preferred_element_type=jnp.float32)  11 us
    dot_general x1, matrix products, local(): recomputed = jnp.dot(hid_bwd, merged, preferred_element_type=jnp.float32)  9.7 us
    dot_general x1, matrix products, scaled_term(): jnp.dot(hid_fwd, merged, preferred_element_type=jnp.float32) * col_scale  8.91 us
    dot_general x1, matrix products, local(): jnp.einsum('td,fd->tf', scaled_cot, merged, preferred_element_type=jnp.fl...  7.7 us
    ppermute x2, starting transfers between devices, from_behind(): return lax.ppermute(array, axis, pairs)  4.65 us
  transfers between devices with their start and end apart: 9, of which 3 were waited for; matrix products, arithmetic and copies ran while one was open for 20% of the time, Pallas kernels for 0%

commit v1 on v0

--- a/solution.py
+++ b/solution.py
@@ -86,7 +86,14 @@
     projected = forward_rows(scaled_term, own_rows)
     section_out = (inflow.astype(jnp.float32) + projected).astype(jnp.bfloat16)
     all_rows = hid_bwd.shape[0]
-    cot_block = lax.all_gather(cotangent, "tensor", axis=0, tiled=True)
+    ring = [cotangent]
+    for hop in range(3):
+        ring.append(lax.ppermute(ring[-1], "tensor", [(dev, (dev + 1) % 4) for dev in range(4)]))
+    cot_block = jnp.roll(
+        jnp.concatenate(ring[::-1], axis=0),
+        (lax.axis_index("tensor") + 1) * ring[0].shape[0],
+        axis=0,
+    )
     scaled_cot = (cot_block.astype(jnp.float32) * col_scale).astype(jnp.bfloat16)
     hid_part = jnp.einsum("td,fd->tf", scaled_cot, merged, preferred_element_type=jnp.float32)
     hid_acc = hid_part

time: 144 us -> 139 us (0.965)
  waiting for transfers between devices: 49.1 us -> 40.7 us
  starting transfers between devices: 6.09 us -> 10 us
  matrix products: 41.4 us -> 43.7 us
  local copies, waits for them, and re-layouts: 5.62 us -> 3.37 us
    all_gather x1 -> x0, waiting for transfers between devices: 27.4 us -> none  [local(): cot_block = lax.all_gather(cotangent, 'tensor', axis=0, tiled=True)]
    ppermute x0 -> x3, waiting for transfers between devices: none -> 11.5 us  [local(): lax.ppermute(ring[-1], 'tensor', [(dev, (dev + 1) % 4) for dev in range(4)])]
    ppermute x2, waiting for transfers between devices: 1.2 us -> 9.02 us  [from_behind(): return lax.ppermute(array, axis, pairs)]
    ppermute x0 -> x3, starting transfers between devices: none -> 3.15 us  [local(): lax.ppermute(ring[-1], 'tensor', [(dev, (dev + 1) % 4) for dev in range(4)])]
    unnamed x28 -> x31, local copies, waits for them, and re-layouts: 4.24 us -> 1.96 us
    dot_general x1, matrix products: 8.91 us -> 10.7 us  [scaled_term(): jnp.dot(hid_fwd, merged, preferred_element_type=jnp.float32) * col_scale]
  transfers between devices with their start and end apart: 9 -> 11, of which waited for: 3 -> 4; matrix products, arithmetic and copies ran while one was open for 20% -> 22% of each run, Pallas kernels for 0% -> 0%
where the time goes in v1:
time: 139 us
  matrix products  43.7 us (31%)
  waiting for transfers between devices  40.7 us (29%)
  blocking collectives  19.6 us (14%)
  between operations  14.3 us (10%)
  starting transfers between devices  10 us (7%)
  other arithmetic  7.07 us (5%)
  local copies, waits for them, and re-layouts  3.37 us (2%)
    reduce_scatter x1, waiting for transfers between devices, forward_rows(): lax.psum_scatter(term_fn(jnp.int32(0), own_rows * lax.axis_size('tensor')...  20.1 us
    psum x1, blocking collectives, column_norms(): return jnp.sqrt(lax.psum(squares, 'tensor') + epsilon)  19.6 us
    ppermute x3, waiting for transfers between devices, local(): lax.ppermute(ring[-1], 'tensor', [(dev, (dev + 1) % 4) for dev in range(4)])  11.5 us
    dot_general x1, matrix products, local(): jnp.einsum('rf,rd->fd', fac_a, fac_b, preferred_element_type=jnp.float32)  10.9 us
    dot_general x1, matrix products, scaled_term(): jnp.dot(hid_fwd, merged, preferred_element_type=jnp.float32) * col_scale  10.7 us
    ppermute x2, waiting for transfers between devices, from_behind(): return lax.ppermute(array, axis, pairs)  9.02 us
    dot_general x1, matrix products, local(): recomputed = jnp.dot(hid_bwd, merged, preferred_element_type=jnp.float32)  8.39 us
    dot_general x1, matrix products, local(): jnp.einsum('td,fd->tf', scaled_cot, merged, preferred_element_type=jnp.fl...  8.01 us
  transfers between devices with their start and end apart: 11, of which 4 were waited for; matrix products, arithmetic and copies ran while one was open for 22% of the time, Pallas kernels for 0%

profile of v1, /device:TPU:0, one launch (start us, length us, event | category | flops | bytes accessed | tf_op | source)
XLA Modules:
  0.0 138.7 jit_solution(6988960764178052782)
XLA Ops:
  7.2 1.3 collective-permute-start.3
  9.6 9.0 %collective-permute-done.3 = bf16[64,2048]{1,0:T(8,128)(2,1)S(1)} collective-permute-done((bf16[64,2048]{1,0:T(8,128)(2,1)}, bf16[64,2048]{1,0:T(8,128)(2,1)S(1)}, u32[]{:S(2)}, u32[]{:S(2)}) %collective-permute-start.3) | collective-permute-done | bytes 262176 | tf_op jit(solution)/shard_map/ppermute | solution.py:16
  18.6 1.0 dynamic-slice_select_fusion
  19.6 1.9 %collective-permute-start.4 = (bf16[64,2048]{1,0:T(8,128)(2,1)S(1)}, bf16[64,2048]{1,0:T(8,128)(2,1)S(1)}, u32[]{:S(2)}, u32[]{:S(2)}) collective-permute-start(bf16[64,2048]{1,0:T(8,128)(2,1)S(1)} %dynamic-slice_select_fusion), channel_id=1, source_target_pairs={{0,1},{1,2},{2,3},{3,0},{4,5},{5,6},{6,7},{7,4},{8,9},{9,10},{10,1... | collective-permute-start | bytes 786440 | tf_op jit(solution)/shard_map/ppermute | solution.py:91
  21.5 0.8 broadcast_select_fusion.5
  22.3 6.6 %collective-permute-done.4 = bf16[64,2048]{1,0:T(8,128)(2,1)S(1)} collective-permute-done((bf16[64,2048]{1,0:T(8,128)(2,1)S(1)}, bf16[64,2048]{1,0:T(8,128)(2,1)S(1)}, u32[]{:S(2)}, u32[]{:S(2)}) %collective-permute-start.4) | collective-permute-done | bytes 262176 | tf_op jit(solution)/shard_map/ppermute | solution.py:91
  29.0 10.9 %multiply_reduce_fusion = (f32[2048]{0:T(1024)S(1)}, bf16[3584,2048]{1,0:T(8,128)(2,1)}) fusion(bf16[1,16,2048]{2,1,0:T(8,128)(2,1)S(1)} %copy-done, bf16[8,3584]{1,0:T(8,128)(2,1)S(1)} %get-tuple-element.13, bf16[8,3584]{1,0:T(8,128)(2,1)S(1)} %get-tuple-element.12, bf16[1,3584,2048]{2,1,0:T(8,128)(2,1)} %param.10), kind=kOutput, calls=%fused_computation.2 | convolution fusion | flops 279148544 | bytes 29548544 | tf_op jit(solution)/shard_map/rf,rd->fd/dot_general | solution.py:74
  39.9 1.3 collective-permute-start.6
  41.2 1.4 broadcast_select_fusion.3
  43.4 4.9 %collective-permute-done.6 = bf16[64,2048]{1,0:T(8,128)(2,1)S(1)} collective-permute-done((bf16[64,2048]{1,0:T(8,128)(2,1)S(1)}, bf16[64,2048]{1,0:T(8,128)(2,1)S(1)}, u32[]{:S(2)}, u32[]{:S(2)}) %collective-permute-start.6) | collective-permute-done | bytes 262176 | tf_op jit(solution)/shard_map/ppermute | solution.py:91
  48.6 8.4 %fusion.5 = f32[2048]{0:T(1024)S(1)} fusion(bf16[3584,2048]{1,0:T(8,128)(2,1)} %get-tuple-element.17, bf16[512,2048]{1,0:T(8,128)(2,1)S(1)} %constant_dynamic-update-slice_fusion, s32[]{:T(128)S(6)} %select_n.91, bf16[128,3584]{1,0:T(8,128)(2,1)S(1)} %get-tuple-element.9, bf16[128,3584]{1,0:T(8,128)(2,1)S(1)} %get-tuple-element.8), kind=kOutput, calls=%fused_computation.14 | convolution fusion | flops 3763337216 | bytes 17571844 | tf_op jit(solution)/shard_map/dot_general | solution.py:103
  57.0 19.6 %all-reduce = (f32[2048]{0:T(1024)S(1)}, f32[2048]{0:T(1024)S(1)}, bf16[256,16]{1,0:T(8,128)(2,1)S(1)}) all-reduce(f32[2048]{0:T(1024)S(1)} %get-tuple-element.16, f32[2048]{0:T(1024)S(1)} %fusion.5, f32[256,16]{1,0:T(8,128)S(1)} %fusion.12), channel_id=1, replica_groups=mesh['section'=8,'tensor'=4] {'tensor'}, use_global_device_ids=true, to_apply=%region_1.2 | all-reduce | flops 8192 | bytes 57344 | tf_op jit(solution)/shard_map/psum | solution.py:20
  76.6 0.6 fusion.18
  77.2 10.7 %convolution_multiply_fusion.1 = f32[256,2048]{1,0:T(8,128)} fusion(bf16[3584,2048]{1,0:T(8,128)(2,1)} %get-tuple-element.17, bf16[128,3584]{1,0:T(8,128)(2,1)} %get-tuple-element.11, bf16[128,3584]{1,0:T(8,128)(2,1)S(1)} %copy-done.7, f32[2048]{0:T(1024)S(1)} %get-tuple-element.15), kind=kOutput, calls=%fused_computation.5 | convolution fusion | flops 3762290688 | bytes 18620416 | tf_op jit(solution)/shard_map/dot_general | solution.py:84
  88.0 8.0 %fusion.7 = f32[256,3584]{1,0:T(8,128)S(1)} fusion(bf16[3584,2048]{1,0:T(8,128)(2,1)} %get-tuple-element.17, f32[2048]{0:T(1024)S(1)} %get-tuple-element.15, bf16[512,2048]{1,0:T(8,128)(2,1)} %copy-done.8, s32[]{:T(128)S(6)} %select_n.91), kind=kOutput, calls=%fused_computation.20 | convolution fusion | flops 3759669248 | bytes 19406852 | tf_op jit(solution)/shard_map/td,fd->tf/dot_general | solution.py:98
  96.0 1.8 %copy-done.1 = f32[256,3584]{1,0:T(8,128)} copy-done((f32[256,3584]{1,0:T(8,128)}, f32[256,3584]{1,0:T(8,128)S(1)}, u32[]{:S(2)}) %copy-start.1) | copy-done | bytes 3670040
  97.8 1.4 %constant_dynamic-slice_fusion = f32[128,3584]{1,0:T(8,128)} fusion(f32[256,3584]{1,0:T(8,128)S(1)} %fusion.7, s32[]{:T(128)S(6)} %select_n.96), kind=kLoop, calls=%fused_computation.48 | loop fusion | bytes 3670020 | tf_op jit(solution)/shard_map/dynamic_slice | solution.py:107
  99.2 4.2 %collective-permute-start = (bf16[64,2048]{1,0:T(8,128)(2,1)S(1)}, bf16[64,2048]{1,0:T(8,128)(2,1)S(1)}, u32[]{:S(2)}, u32[]{:S(2)}) collective-permute-start(bf16[64,2048]{1,0:T(8,128)(2,1)S(1)} %bitcast.41), channel_id=1, source_target_pairs={{0,8},{4,12},{8,16},{12,20},{16,24},{20,28},{1,9},{5,13},{9,17},{1... | collective-permute-start | bytes 786440 | tf_op jit(solution)/shard_map/ppermute | solution.py:16
  103.4 1.7 %fusion.10 = f32[256,16]{0,1:T(8,128)S(1)} fusion(f32[2048]{0:T(1024)S(1)} %get-tuple-element.15, bf16[512,2048]{1,0:T(8,128)(2,1)} %copy-done.8, s32[]{:T(128)S(6)} %select_n.91, bf16[1,16,2048]{2,1,0:T(8,128)(2,1)S(1)} %copy-done), kind=kOutput, calls=%fused_computation.21 | convolution fusion | flops 18350080 | bytes 1138692 | tf_op jit(solution)/shard_map/td,rd->tr/dot_general | solution.py:100
  105.4 2.3 %convolution_bitcast_fusion.1 = f32[1,16,2048]{2,1,0:T(8,128)} fusion(f32[2048]{0:T(1024)S(1)} %get-tuple-element.15, bf16[512,2048]{1,0:T(8,128)(2,1)} %copy-done.8, s32[]{:T(128)S(6)} %select_n.91, bf16[256,16]{1,0:T(8,128)(2,1)S(1)} %get-tuple-element.7), kind=kOutput, calls=%fused_computation.7 | convolution fusion | flops 18350080 | bytes 1196036 | tf_op jit(solution)/shard_map/tr,td->rd/dot_general | solution.py:102
  107.7 1.0 convolution_bitcast_fusion
  108.7 1.2 fusion.6
  109.9 20.1 %reduce-scatter.2.cloned.1.call-done = f32[64,2048]{1,0:T(8,128)} async-done(((f32[256,2048]{1,0:T(8,128)}), f32[64,2048]{1,0:T(8,128)}) %reduce-scatter.2.cloned.1.call-update) | async-done | bytes 524304 | tf_op jit(solution)/shard_map/reduce_scatter | solution.py:24
  130.0 1.8 %fusion.13 = bf16[1,64,2048]{2,1,0:T(8,128)(2,1)} fusion(f32[64,2048]{1,0:T(8,128)} %reduce-scatter.2.cloned.1.call-done, bf16[64,2048]{1,0:T(8,128)(2,1)S(1)} %collective-permute-done, bf16[64,4096]{1,0:T(8,128)(2,1)S(1)} %copy-done.9, s32[]{:T(128)S(6)} %select_n.80, pred[]{:T(512)S(6)} %lt.34), kind=kLoop, calls=%fused_computation.24 | loop fusion | flops 524288 | bytes 1310725 | tf_op jit(solution)/shard_map/broadcast_in_dim | solution.py:116
  (48 shorter events, 2.4 us)
Async XLA Ops:
  7.2 21.8 %copy-start = (bf16[1,16,2048]{2,1,0:T(8,128)(2,1)S(1)}, bf16[1,16,2048]{2,1,0:T(8,128)(2,1)}, u32[]{:S(2)}) copy-start(bf16[1,16,2048]{2,1,0:T(8,128)(2,1)} %param.12) | copy-start | bytes 196612
  7.2 122.8 %reduce-scatter.2.cloned.1.call-start = ((), (), s32[]{:S(2)}) async-start(), calls=%async_computation.1 | async-start | bytes 2621440 | tf_op jit(solution)/shard_map/reduce_scatter | solution.py:24
  7.2 11.4 %collective-permute-start.3 = (bf16[64,2048]{1,0:T(8,128)(2,1)}, bf16[64,2048]{1,0:T(8,128)(2,1)S(1)}, u32[]{:S(2)}, u32[]{:S(2)}) collective-permute-start(bf16[64,2048]{1,0:T(8,128)(2,1)} %bitcast.40), channel_id=1, source_target_pairs={{8,0},{12,4},{16,8},{20,12},{24,16},{28,20},{9,1},{13,5},{17,9},{2... | collective-permute-start | bytes 786440 | tf_op jit(solution)/shard_map/ppermute | solution.py:16
  8.5 13.0 %collective-permute-start.2 = (bf16[8,3584]{1,0:T(8,128)(2,1)}, bf16[8,3584]{1,0:T(8,128)(2,1)S(1)}, u32[]{:S(2)}, u32[]{:S(2)}) collective-permute-start(bf16[8,3584]{1,0:T(8,128)(2,1)} %bitcast.37), channel_id=1, source_target_pairs={{0,4},{4,0},{8,12},{12,8},{16,20},{20,16},{24,28},{28,24},{1,5},{5... | collective-permute-start | bytes 172040 | tf_op jit(solution)/shard_map/ppermute | solution.py:10
  9.1 32.1 %collective-permute-start.1 = (bf16[128,3584]{1,0:T(8,128)(2,1)}, bf16[128,3584]{1,0:T(8,128)(2,1)S(1)}, u32[]{:S(2)}, u32[]{:S(2)}) collective-permute-start(bf16[128,3584]{1,0:T(8,128)(2,1)} %bitcast.35), channel_id=1, source_target_pairs={{0,4},{4,0},{8,12},{12,8},{16,20},{20,16},{24,28},{28,24},{1,5},{5... | collective-permute-start | bytes 2752520 | tf_op jit(solution)/shard_map/ppermute | solution.py:10
  9.2 33.4 %collective-permute-start.7 = (bf16[128,3584]{1,0:T(8,128)(2,1)}, bf16[128,3584]{1,0:T(8,128)(2,1)S(1)}, u32[]{:S(2)}, u32[]{:S(2)}) collective-permute-start(bf16[128,3584]{1,0:T(8,128)(2,1)} %bitcast.36), channel_id=1, source_target_pairs={{0,4},{4,0},{8,12},{12,8},{16,20},{20,16},{24,28},{28,24},{1,5},{5... | collective-permute-start | bytes 2752520 | tf_op jit(solution)/shard_map/ppermute | solution.py:10
  19.6 9.3 %collective-permute-start.4 = (bf16[64,2048]{1,0:T(8,128)(2,1)S(1)}, bf16[64,2048]{1,0:T(8,128)(2,1)S(1)}, u32[]{:S(2)}, u32[]{:S(2)}) collective-permute-start(bf16[64,2048]{1,0:T(8,128)(2,1)S(1)} %dynamic-slice_select_fusion), channel_id=1, source_target_pairs={{0,1},{1,2},{2,3},{3,0},{4,5},{5,6},{6,7},{7,4},{8,9},{9,10},{10,1... | collective-permute-start | bytes 786440 | tf_op jit(solution)/shard_map/ppermute | solution.py:91
  29.0 11.0 %collective-permute-start.5 = (bf16[64,2048]{1,0:T(8,128)(2,1)S(1)}, bf16[64,2048]{1,0:T(8,128)(2,1)S(1)}, u32[]{:S(2)}, u32[]{:S(2)}) collective-permute-start(bf16[64,2048]{1,0:T(8,128)(2,1)S(1)} %collective-permute-done.4), channel_id=1, source_target_pairs={{0,1},{1,2},{2,3},{3,0},{4,5},{5,6},{6,7},{7,4},{8,9},{9,10},{10,1... | collective-permute-start | bytes 786440 | tf_op jit(solution)/shard_map/ppermute | solution.py:91
  29.0 12.2 %copy-start.3 = (bf16[1,128,3584]{2,1,0:T(8,128)(2,1)S(1)}, bf16[1,128,3584]{2,1,0:T(8,128)(2,1)}, u32[]{:S(2)}) copy-start(bf16[1,128,3584]{2,1,0:T(8,128)(2,1)} %param.14) | copy-start | bytes 2752516
  39.9 2.7 %copy-start.4 = (bf16[1,128,3584]{2,1,0:T(8,128)(2,1)S(1)}, bf16[1,128,3584]{2,1,0:T(8,128)(2,1)}, u32[]{:S(2)}) copy-start(bf16[1,128,3584]{2,1,0:T(8,128)(2,1)} %param.17) | copy-start | bytes 2752516
  39.9 8.4 %collective-permute-start.6 = (bf16[64,2048]{1,0:T(8,128)(2,1)S(1)}, bf16[64,2048]{1,0:T(8,128)(2,1)S(1)}, u32[]{:S(2)}, u32[]{:S(2)}) collective-permute-start(bf16[64,2048]{1,0:T(8,128)(2,1)S(1)} %collective-permute-done.5), channel_id=1, source_target_pairs={{0,1},{1,2},{2,3},{3,0},{4,5},{5,6},{6,7},{7,4},{8,9},{9,10},{10,1... | collective-permute-start | bytes 786440 | tf_op jit(solution)/shard_map/ppermute | solution.py:91
  42.8 5.7 %copy-start.5 = (bf16[128,3584]{1,0:T(8,128)(2,1)}, bf16[128,3584]{1,0:T(8,128)(2,1)S(1)}, u32[]{:S(2)}) copy-start(bf16[128,3584]{1,0:T(8,128)(2,1)S(1)} %get-tuple-element.9) | copy-start | bytes 2752516
  48.5 8.4 %copy-start.8 = (bf16[512,2048]{1,0:T(8,128)(2,1)}, bf16[512,2048]{1,0:T(8,128)(2,1)S(1)}, u32[]{:S(2)}) copy-start(bf16[512,2048]{1,0:T(8,128)(2,1)S(1)} %constant_dynamic-update-slice_fusion) | copy-start | bytes 6291460
  48.6 28.0 %copy-start.10 = (f32[1,2048]{1,0:T(1,128)S(1)}, f32[1,2048]{1,0:T(1,128)}, u32[]{:S(2)}) copy-start(f32[1,2048]{1,0:T(1,128)} %param.13) | copy-start | bytes 24580
  48.6 28.6 %copy-start.7 = (bf16[128,3584]{1,0:T(8,128)(2,1)S(1)}, bf16[128,3584]{1,0:T(8,128)(2,1)}, u32[]{:S(2)}) copy-start(bf16[128,3584]{1,0:T(8,128)(2,1)} %get-tuple-element.10) | copy-start | bytes 2752516
  96.0 1.8 %copy-start.1 = (f32[256,3584]{1,0:T(8,128)}, f32[256,3584]{1,0:T(8,128)S(1)}, u32[]{:S(2)}) copy-start(f32[256,3584]{1,0:T(8,128)S(1)} %fusion.7) | copy-start | bytes 11010052
  97.8 1.4 %copy-start.11 = (bf16[1,64,2048]{2,1,0:T(8,128)(2,1)S(1)}, bf16[1,64,2048]{2,1,0:T(8,128)(2,1)}, u32[]{:S(2)}) copy-start(bf16[1,64,2048]{2,1,0:T(8,128)(2,1)} %param.15) | copy-start | bytes 786436
  99.2 9.5 %collective-permute-start.9 = (f32[128,3584]{1,0:T(8,128)}, f32[128,3584]{1,0:T(8,128)S(1)}, u32[]{:S(2)}, u32[]{:S(2)}) collective-permute-start(f32[128,3584]{1,0:T(8,128)} %constant_dynamic-slice_fusion), channel_id=1, source_target_pairs={{0,4},{4,0},{8,12},{12,8},{16,20},{20,16},{24,28},{28,24},{1,5},{5... | collective-permute-start | bytes 5505032 | tf_op jit(solution)/shard_map/ppermute | solution.py:10
  99.2 10.7 %collective-permute-start = (bf16[64,2048]{1,0:T(8,128)(2,1)S(1)}, bf16[64,2048]{1,0:T(8,128)(2,1)S(1)}, u32[]{:S(2)}, u32[]{:S(2)}) collective-permute-start(bf16[64,2048]{1,0:T(8,128)(2,1)S(1)} %bitcast.41), channel_id=1, source_target_pairs={{0,8},{4,12},{8,16},{12,20},{16,24},{20,28},{1,9},{5,13},{9,17},{1... | collective-permute-start | bytes 786440 | tf_op jit(solution)/shard_map/ppermute | solution.py:16
  103.4 4.3 %copy-start.6 = (bf16[128,3584]{1,0:T(8,128)(2,1)S(1)}, bf16[128,3584]{1,0:T(8,128)(2,1)}, u32[]{:S(2)}) copy-start(bf16[128,3584]{1,0:T(8,128)(2,1)} %copy-done.5) | copy-start | bytes 2752516
  105.1 3.6 %copy-start.2 = (f32[256,3584]{1,0:T(8,128)S(1)}, f32[256,3584]{1,0:T(8,128)}, u32[]{:S(2)}) copy-start(f32[256,3584]{1,0:T(8,128)} %copy-done.1) | copy-start | bytes 11010052
  105.1 2.6 %collective-permute-start.8 = (f32[256,16]{0,1:T(8,128)S(1)}, f32[256,16]{0,1:T(8,128)S(1)}, u32[]{:S(2)}, u32[]{:S(2)}) collective-permute-start(f32[256,16]{0,1:T(8,128)S(1)} %fusion.10), channel_id=1, source_target_pairs={{0,4},{4,0},{8,12},{12,8},{16,20},{20,16},{24,28},{28,24},{1,5},{5... | collective-permute-start | bytes 49160 | tf_op jit(solution)/shard_map/ppermute | solution.py:10
  108.7 21.3 %copy-start.9 = (bf16[64,4096]{1,0:T(8,128)(2,1)S(1)}, bf16[64,4096]{1,0:T(8,128)(2,1)}, u32[]{:S(2)}) copy-start(bf16[64,4096]{1,0:T(8,128)(2,1)} %param.16) | copy-start | bytes 1572868
Sparse Core Ops, SparseCore 0:
  88.1 41.8 reduce-scatter.1
